TPU v7x, 32 devices: a whole 2x2x4 slice. The times are simulated.
32 devices in a mesh: genome: 4 (over z), trow: 2 (over core), tcol: 4 (over y, x).
Axes of the slice: x: 2, y: 2, z: 4, core: 2. Of those that a mesh axis runs over, the one named last changes fastest.
Arguments:
- ldscore: float32 [4096], P('genome'), may hold values from 1 to 100
- zscores: bfloat16 [4096, 4096], P('genome', ('trow', 'tcol')), may hold values from -30 to 30
Outputs:
- rg: float32 [2, 2048, 2, 2048], P('trow', 'genome', None, 'tcol')
- rg_se: float32 [2, 2048, 2, 2048], P('trow', 'genome', None, 'tcol')
All inputs are finite; a program needn't handle non-finite values.
Results may differ from a plain program's by a relative error of at most 0.038.
Values may be sent and summed in bfloat16 or wider, within the bound.
No kernel may reach another device: no remote copies, remote signals or barrier semaphores. Data moves between devices by JAX's collectives and lax.ppermute only.
A program may use at most 192 MiB of HBM per device.

v0:
```python
import jax
import jax.numpy as jnp
from jax import lax
from jax.sharding import PartitionSpec as P

floor_value = 0.002


def contract(left, right):
    return lax.dot_general(
        left, right, (((0,), (0,)), ((), ())), preferred_element_type=jnp.float32
    )


def slope_fit(inv_sum, ld_sum, y_sum, l_sum, count):
    return (inv_sum * l_sum - count * y_sum) / (inv_sum * ld_sum - count * count)


def weights_for(herit_pos, ld_column):
    return (1.0 / (1.0 + herit_pos[None, :] * ld_column[:, None])).astype(jnp.bfloat16)


def coupling(tiles):
    return (tiles[2] * tiles[1] - tiles[3] * tiles[0]) / (tiles[2] * tiles[4] - tiles[3] * tiles[3])


def per_device(ldscore, zscores):
    blocks = lax.axis_size("genome")
    grid_rows = lax.axis_size("trow")
    grid_cols = lax.axis_size("tcol")
    snp_count = zscores.shape[0]
    shard_width = zscores.shape[1]
    traits = shard_width * grid_rows * grid_cols
    row_width = traits // grid_rows
    row_share = row_width // blocks
    row_index = lax.axis_index("trow")
    col_index = lax.axis_index("tcol")
    genome_index = lax.axis_index("genome")
    ld_weight = 1.0 / ldscore
    z_float = zscores.astype(jnp.float32)
    z_square = z_float * z_float
    own_stats = jnp.stack(
        [jnp.sum(z_square * ld_weight[:, None], axis=0), jnp.sum(z_square, axis=0)]
    )
    own_scalars = jnp.stack([jnp.sum(ld_weight), jnp.sum(ldscore)])
    all_stats, all_scalars = (
        lax.all_gather(own_stats[None], ("genome", "trow", "tcol"), axis=0, tiled=True),
        lax.all_gather(own_scalars[None], ("genome", "trow", "tcol"), axis=0, tiled=True),
    )
    all_stats = all_stats.reshape(blocks, grid_rows * grid_cols, 2, shard_width)
    all_stats = all_stats.transpose(0, 2, 1, 3).reshape(blocks, 2, traits)
    all_scalars = all_scalars.reshape(blocks, grid_rows * grid_cols, 2)[:, 0, :]
    total_stats = jnp.sum(all_stats, axis=0)
    total_scalars = jnp.sum(all_scalars, axis=0)
    herit_full = slope_fit(
        total_scalars[0],
        total_scalars[1],
        total_stats[0],
        total_stats[1],
        float(snp_count * blocks),
    )
    rest_stats = total_stats[None] - all_stats
    rest_scalars = total_scalars[None] - all_scalars
    herit_del = slope_fit(
        rest_scalars[:, 0:1],
        rest_scalars[:, 1:2],
        rest_stats[:, 0],
        rest_stats[:, 1],
        float(snp_count * (blocks - 1)),
    )
    herit_pos = jnp.maximum(herit_full, 0.0)
    col_z = lax.all_gather(zscores, "trow", axis=1, tiled=True)
    col_herit = lax.dynamic_index_in_dim(
        herit_pos.reshape(grid_rows, grid_cols, shard_width), col_index, 1, keepdims=False
    ).reshape(-1)
    col_u = weights_for(col_herit, ldscore)
    col_zu = (col_z.astype(jnp.float32) * col_u.astype(jnp.float32)).astype(jnp.bfloat16)
    piece = lax.all_gather(zscores, "tcol", axis=1, tiled=True)
    herit_rows = lax.dynamic_slice_in_dim(herit_pos, row_index * row_width, piece.shape[1])
    row_u = weights_for(herit_rows, ldscore)
    u_float = row_u.astype(jnp.float32)
    scaled = piece.astype(jnp.float32) * u_float
    row_zu = scaled.astype(jnp.bfloat16)
    row_scaled = (scaled * ld_weight[:, None]).astype(jnp.bfloat16)
    products = [contract(row_scaled, col_zu), contract(row_zu, col_zu)]
    row_inv = (u_float * ld_weight[:, None]).astype(jnp.bfloat16)
    row_ld = (u_float * ldscore[:, None]).astype(jnp.bfloat16)
    products = products + [
        contract(row_inv, col_u),
        contract(row_u, col_u),
        contract(row_ld, col_u),
    ]
    sums = jnp.stack(products)
    sums = sums.astype(jnp.bfloat16)[:, None]
    row_start = row_index * row_width + genome_index * row_share
    tiles = lax.all_to_all(sums, "genome", split_axis=2, concat_axis=1, tiled=True)
    tile_values = tiles.astype(jnp.float32)
    totals = jnp.sum(tile_values, axis=1)
    deleted = totals[:, None] - tile_values
    full_g = coupling(totals)
    del_g = coupling(deleted)
    herit_floor = jnp.maximum(herit_full, floor_value)
    del_floor = jnp.maximum(herit_del, floor_value)
    rows_full = lax.dynamic_slice_in_dim(herit_floor, row_start, row_share)
    cols_full = lax.dynamic_index_in_dim(
        herit_floor.reshape(grid_rows, grid_cols, shard_width), col_index, 1, keepdims=False
    ).reshape(-1)
    rows_del = lax.dynamic_slice_in_dim(del_floor, row_start, row_share, axis=1)
    cols_del = lax.dynamic_index_in_dim(
        del_floor.reshape(blocks, grid_rows, grid_cols, shard_width), col_index, 2, keepdims=False
    ).reshape(blocks, -1)
    rg_tile = full_g / jnp.sqrt(rows_full[:, None] * cols_full[None, :])
    rg_del = del_g / jnp.sqrt(rows_del[:, :, None] * cols_del[:, None, :])
    mean_del = jnp.mean(rg_del, axis=0)
    differ = rg_del - mean_del[None]
    spread = jnp.sum(differ * differ, axis=0)
    se_tile = jnp.sqrt((blocks - 1) / blocks * spread)
    out_shape = (1, row_share, grid_rows, shard_width)
    return (rg_tile.reshape(out_shape), se_tile.reshape(out_shape))


def solution(mesh):
    return jax.shard_map(
        per_device,
        mesh=mesh,
        in_specs=(P("genome"), P("genome", ("trow", "tcol"))),
        out_specs=(P("trow", "genome", None, "tcol"), P("trow", "genome", None, "tcol")),
        check_vma=False,
    )
```

profile of v0, /device:TPU:0, one launch (start us, length us, event | category | flops | bytes accessed | tf_op | source)
XLA Modules:
  0.0 1032.2 jit_solution(11515729871586139848)
XLA Ops:
  7.9 0.7 all-gather.6.cloned.1.call-update
  8.7 1.3 fusion.41
  10.0 1.5 maximum_dynamic-update-slice_fusion
  11.4 42.1 %all-reduce = f32[64]{0:T(128)S(1)} all-reduce(f32[64]{0:T(128)S(1)} %maximum_dynamic-update-slice_fusion), channel_id=2, replica_groups=mesh['genome'=4,'trow'=2,'tcol'=4] {'genome','trow','tcol'}, use_global_device_ids=true, to_apply=%add | all-reduce | flops 64 | bytes 512
  55.5 1.6 multiply_reduce_fusion.1
  57.2 67.2 %all-gather.2 = f32[32,2,512]{2,1,0:T(2,128)S(1)} all-gather(f32[1,2,512]{2,1,0:T(2,128)S(1)} %maximum_bitcast_fusion), channel_id=3, replica_groups=mesh['genome'=4,'trow'=2,'tcol'=4] {'genome','trow','tcol'}, dimensions={0}, use_global_device_ids=true | all-gather | bytes 135168 | tf_op jit(solution)/shard_map/all_gather | solution.py:47
  125.3 10.8 %bitcast_dynamic-update-slice_fusion.4 = bf16[5,1,2048,1024]{3,2,1,0:T(8,128)(2,1)} fusion(bf16[1024,2048]{1,0:T(8,128)(2,1)} %all-gather.6.cloned.1.call-done, f32[1024]{0:T(1024)S(1)} %get-tuple-element.21, f32[1024]{0:T(1024)} %param.2, f32[2048]{0:T(1024)S(1)} %dynamic_slice.20, bf16[1024,1024]{1,0:T(8,128)(2,1)} %all-gather.8.cloned.1.call-done, ...), kind=kOutput, calls=%fused_computation.27 | convolution fusion | flops 4324327424 | bytes 10510336 | tf_op jit(solution)/shard_map/dot_general | solution.py:10
  136.1 7.8 bitcast_dynamic-update-slice_fusion.3
  143.9 7.7 bitcast_dynamic-update-slice_fusion.2
  151.6 6.9 bitcast_dynamic-update-slice_fusion.1
  158.5 6.8 bitcast_dynamic-update-slice_fusion
  165.3 23.9 %copy.21 = bf16[5,1,2048,1024]{3,0,1,2:T(8,128)(2,1)} copy(bf16[5,1,2048,1024]{3,2,1,0:T(8,128)(2,1)} %bitcast_dynamic-update-slice_fusion) | data formatting | bytes 41943040 | tf_op jit(solution)/shard_map/stack | solution.py:93
  189.2 9.9 all-to-all-start
  200.0 1.1 slice_multiply_fusion.6
  201.8 715.7 %all-to-all-done = bf16[5,1,2048,1024]{3,0,1,2:T(8,128)(2,1)} async-done(((bf16[5,1,2048,1024]{3,0,1,2:T(8,128)(2,1)}), bf16[5,1,2048,1024]{3,0,1,2:T(8,128)(2,1)}, u32[]{:S(2)}, u32[]{:S(2)}) %all-to-all-start) | async-done | bytes 20971552 | tf_op jit(solution)/shard_map/all_to_all | solution.py:96
  917.5 26.6 %copy.22 = bf16[5,1,2048,1024]{3,2,0,1:T(8,128)(2,1)} copy(bf16[5,1,2048,1024]{3,0,1,2:T(8,128)(2,1)} %all-to-all-done) | data formatting | bytes 41943040 | tf_op jit(solution)/shard_map/all_to_all | solution.py:96
  944.1 16.0 %convert_reduce_fusion = f32[5,512,1024]{2,1,0:T(8,128)} fusion(bf16[5,4,512,1024]{3,2,1,0:T(8,128)(2,1)} %bitcast.61), kind=kLoop, calls=%fused_computation.1 | loop fusion | flops 18350080 | bytes 31457280 | tf_op jit(solution)/shard_map/reduce_sum | solution.py:98
  960.1 28.2 %convert_subtract_fusion = f32[5,4,512,1024]{3,2,1,0:T(8,128)} fusion(bf16[5,4,512,1024]{3,2,1,0:T(8,128)(2,1)} %bitcast.62, f32[5,512,1024]{2,1,0:T(8,128)} %convert_reduce_fusion), kind=kLoop, calls=%fused_computation | loop fusion | flops 20971520 | bytes 73400320 | tf_op jit(solution)/shard_map/sub | solution.py:99
  988.3 2.6 fusion.26
  990.8 20.1 %fusion.44 = (f32[512,1024]{1,0:T(8,128)S(1)}, f32[4,512,1024]{2,1,0:T(8,128)}) fusion(f32[4,1024]{1,0:T(4,128)S(1)} %bitcast.71, f32[4,512]{1,0:T(4,128)S(1)} %fusion.33, f32[5,4,512,1024]{3,2,1,0:T(8,128)} %convert_subtract_fusion), kind=kLoop, calls=%fused_computation.85 | loop fusion | flops 20447232 | bytes 52453376 | tf_op jit(solution)/shard_map/reduce_sum | solution.py:114
  1011.1 5.1 multiply_reduce_fusion
  1016.7 2.8 sqrt.22
  1019.5 3.0 div.75
  1022.6 2.6 rsqrt_multiply_fusion
  (47 shorter events, 4.4 us)
Async XLA Ops:
  7.2 118.0 %all-gather.8.cloned.1.call-start = ((), (), s32[]{:S(2)}) async-start(), calls=%async_computation.2 | async-start | bytes 3145728 | tf_op jit(solution)/shard_map/all_gather | solution.py:72
  7.9 117.3 %all-gather.6.cloned.1.call-start = ((), (), s32[]{:S(2)}) async-start(), calls=%async_computation.1 | async-start | bytes 5242880 | tf_op jit(solution)/shard_map/all_gather | solution.py:78
  125.2 10.9 %copy-start.1 = (f32[1024]{0:T(1024)S(1)}, f32[1024]{0:T(1024)}, u32[]{:S(2)}) copy-start(f32[1024]{0:T(1024)} %param.2) | copy-start | bytes 12292
  125.2 10.9 %copy-start.2 = (bf16[1024,2048]{1,0:T(8,128)(2,1)S(1)}, bf16[1024,2048]{1,0:T(8,128)(2,1)}, u32[]{:S(2)}) copy-start(bf16[1024,2048]{1,0:T(8,128)(2,1)} %all-gather.6.cloned.1.call-done) | copy-start | bytes 12582916
  125.3 10.9 %copy-start.3 = (bf16[1024,1024]{1,0:T(8,128)(2,1)S(1)}, bf16[1024,1024]{1,0:T(8,128)(2,1)}, u32[]{:S(2)}) copy-start(bf16[1024,1024]{1,0:T(8,128)(2,1)} %all-gather.8.cloned.1.call-done) | copy-start | bytes 6291460
  189.2 728.2 %all-to-all-start = ((bf16[5,1,2048,1024]{3,0,1,2:T(8,128)(2,1)}), bf16[5,1,2048,1024]{3,0,1,2:T(8,128)(2,1)}, u32[]{:S(2)}, u32[]{:S(2)}) async-start(bf16[5,1,2048,1024]{3,0,1,2:T(8,128)(2,1)} %copy.21), calls=%async_computation | async-start | bytes 67108864 | tf_op jit(solution)/shard_map/all_to_all | solution.py:96
  960.1 28.2 %copy-start = (f32[5,512,1024]{2,1,0:T(8,128)S(1)}, f32[5,512,1024]{2,1,0:T(8,128)}, u32[]{:S(2)}) copy-start(f32[5,512,1024]{2,1,0:T(8,128)} %convert_reduce_fusion) | copy-start | bytes 31457284
Sparse Core Ops, SparseCore 0:
  9.5 13.2 all-gather.7
  24.7 54.7 all-gather.5
where the time goes:
time: 1040 us; the launch traced here: 1030 us
  waiting for transfers between devices  717 us (69%)
  blocking collectives  109 us (10%)
  other arithmetic  81.7 us (8%)
  local copies, waits for them, and re-layouts  58.2 us (6%)
  matrix products  40 us (4%)
  between operations  15.8 us (2%)
    all_to_all x1, waiting for transfers between devices, per_device(): lax.all_to_all(sums, 'genome', split_axis=2, concat_axis=1, tiled=True)  716 us
    all_gather x1, blocking collectives, per_device(): lax.all_gather(own_stats[None], ('genome', 'trow', 'tcol'), axis=0, tiled...  67.2 us
    unnamed x1, blocking collectives  42.1 us
    dot_general x5, matrix products, contract(): lax.dot_general(left, right, (((0,), (0,)), ((), ())), preferred_element_...  40 us
    sub x1, other arithmetic, per_device(): deleted = totals[:, None] - tile_values  28.2 us
    all_to_all x1, local copies, waits for them, and re-layouts, per_device(): lax.all_to_all(sums, 'genome', split_axis=2, concat_axis=1, tiled=True)  26.6 us
    another operation x1, local copies, waits for them, and re-layouts, per_device(): sums = jnp.stack(products)  23.9 us
  transfers between devices with their start and end apart: 3, of which 1 were waited for; matrix products, arithmetic and copies ran while one was open for 1% of the time, Pallas kernels for 0%

commit v1 on v0

--- a/solution.py
+++ b/solution.py
@@ -93,7 +93,10 @@
     sums = jnp.stack(products)
     sums = sums.astype(jnp.bfloat16)[:, None]
     row_start = row_index * row_width + genome_index * row_share
-    tiles = lax.all_to_all(sums, "genome", split_axis=2, concat_axis=1, tiled=True)
+    tiles = jnp.concatenate(
+        lax.all_to_all(jnp.stack(jnp.split(sums, lax.axis_size("genome"), axis=2)), "genome", 0, 0),
+        axis=1,
+    )
     tile_values = tiles.astype(jnp.float32)
     totals = jnp.sum(tile_values, axis=1)
     deleted = totals[:, None] - tile_values

time: 1040 us -> 739 us (0.71)
  waiting for transfers between devices: 717 us -> 448 us
  local copies, waits for them, and re-layouts: 58.2 us -> 18.7 us
    all_to_all x1, waiting for transfers between devices: 716 us -> 446 us  [per_device(): lax.all_to_all(jnp.stack(jnp.split(sums, lax.axis_size('genome'), axis=2)...]
    all_to_all x1 -> x0, local copies, waits for them, and re-layouts: 26.6 us -> none  [per_device(): lax.all_to_all(sums, 'genome', split_axis=2, concat_axis=1, tiled=True)]
    another operation x1 -> x2, local copies, waits for them, and re-layouts: 23.9 us -> 10.3 us  [per_device(): jnp.stack(jnp.split(sums, lax.axis_size('genome'), axis=2))]
where the time goes in v1:
time: 739 us; the launch traced here: 729 us
  waiting for transfers between devices  448 us (61%)
  blocking collectives  109 us (15%)
  other arithmetic  90 us (12%)
  matrix products  39.7 us (5%)
  local copies, waits for them, and re-layouts  18.7 us (3%)
  between operations  16 us (2%)
  starting transfers between devices  8.04 us (1%)
    all_to_all x1, waiting for transfers between devices, per_device(): lax.all_to_all(jnp.stack(jnp.split(sums, lax.axis_size('genome'), axis=2)...  446 us
    all_gather x1, blocking collectives, per_device(): lax.all_gather(own_stats[None], ('genome', 'trow', 'tcol'), axis=0, tiled...  67.3 us
    unnamed x1, blocking collectives  42.1 us
    dot_general x5, matrix products, contract(): lax.dot_general(left, right, (((0,), (0,)), ((), ())), preferred_element_...  39.7 us
    sub x1, other arithmetic, per_device(): deleted = totals[:, None] - tile_values  23.2 us
    reduce_sum x1, other arithmetic, per_device(): mean_del = jnp.mean(rg_del, axis=0)  19.9 us
    reduce_sum x1, other arithmetic, per_device(): totals = jnp.sum(tile_values, axis=1)  16 us
  transfers between devices with their start and end apart: 3, of which 1 were waited for; matrix products, arithmetic and copies ran while one was open for 1% of the time, Pallas kernels for 0%

profile of v1, /device:TPU:0, one launch (start us, length us, event | category | flops | bytes accessed | tf_op | source)
XLA Modules:
  0.0 729.3 jit_solution(6737334093491915948)
XLA Ops:
  8.7 1.3 fusion.41
  10.0 1.5 maximum_dynamic-update-slice_fusion
  11.4 42.1 %all-reduce = f32[64]{0:T(128)S(1)} all-reduce(f32[64]{0:T(128)S(1)} %maximum_dynamic-update-slice_fusion), channel_id=2, replica_groups=mesh['genome'=4,'trow'=2,'tcol'=4] {'genome','trow','tcol'}, use_global_device_ids=true, to_apply=%add | all-reduce | flops 64 | bytes 512
  53.6 1.6 multiply_reduce_fusion.1
  55.3 67.3 %all-gather.2 = f32[32,2,512]{2,1,0:T(2,128)S(1)} all-gather(f32[1,2,512]{2,1,0:T(2,128)S(1)} %maximum_bitcast_fusion), channel_id=3, replica_groups=mesh['genome'=4,'trow'=2,'tcol'=4] {'genome','trow','tcol'}, dimensions={0}, use_global_device_ids=true | all-gather | bytes 135168 | tf_op jit(solution)/shard_map/all_gather | solution.py:47
  125.4 10.8 %bitcast_dynamic-update-slice_fusion.4 = bf16[5,1,2048,1024]{3,2,1,0:T(8,128)(2,1)} fusion(bf16[1024,2048]{1,0:T(8,128)(2,1)} %all-gather.6.cloned.1.call-done, f32[1024]{0:T(1024)S(1)} %get-tuple-element.24, f32[1024]{0:T(1024)} %param.2, f32[2048]{0:T(1024)S(1)} %dynamic_slice.20, bf16[1024,1024]{1,0:T(8,128)(2,1)} %all-gather.8.cloned.1.call-done, ...), kind=kOutput, calls=%fused_computation.34 | convolution fusion | flops 4324327424 | bytes 10510336 | tf_op jit(solution)/shard_map/dot_general | solution.py:10
  136.3 7.8 %bitcast_dynamic-update-slice_fusion.3 = bf16[5,1,2048,1024]{3,2,1,0:T(8,128)(2,1)} fusion(bf16[5,1,2048,1024]{3,2,1,0:T(8,128)(2,1)} %bitcast_dynamic-update-slice_fusion.4, bf16[1024,2048]{1,0:T(8,128)(2,1)S(1)} %copy-done.2, f32[1024]{0:T(1024)S(1)} %copy-done.1, f32[2048]{0:T(1024)S(1)} %dynamic_slice.20, bf16[1024,1024]{1,0:T(8,128)(2,1)S(1)} %copy-done.3, ...), kind=kOutput, calls=%fused_computation.33 | convolution fusion | flops 4322230272 | bytes 10506240 | tf_op jit(solution)/shard_map/dot_general | solution.py:10
  144.1 7.4 %bitcast_dynamic-update-slice_fusion.2 = bf16[5,1,2048,1024]{3,2,1,0:T(8,128)(2,1)} fusion(bf16[5,1,2048,1024]{3,2,1,0:T(8,128)(2,1)} %bitcast_dynamic-update-slice_fusion.3, f32[1024]{0:T(1024)S(1)} %get-tuple-element.24, f32[1024]{0:T(1024)S(1)} %copy-done.1, f32[2048]{0:T(1024)S(1)} %dynamic_slice.20, f32[1024]{0:T(1024)S(1)} %bitcast.90), kind=kOutput, calls=%fused_computation.32 | convolution fusion | flops 4315938816 | bytes 4218880 | tf_op jit(solution)/shard_map/dot_general | solution.py:10
  151.5 6.9 bitcast_dynamic-update-slice_fusion.1
  158.3 6.8 bitcast_dynamic-update-slice_fusion
  165.2 3.1 slice_bitcast_fusion
  168.2 7.2 slice_bitcast_fusion.3
  175.5 8.8 %pad_maximum_fusion = bf16[4,5,1,512,1024]{4,3,1,2,0:T(8,128)(2,1)} fusion(bf16[1,5,1,512,1024]{4,3,1,2,0:T(8,128)(2,1)S(1)} %slice_bitcast_fusion, bf16[1,5,1,512,1024]{4,3,1,2,0:T(8,128)(2,1)S(1)} %get-tuple-element.15, bf16[1,5,1,512,1024]{4,3,1,2,0:T(8,128)(2,1)S(1)} %get-tuple-element.16, bf16[1,5,1,512,1024]{4,3,1,2,0:T(8,128)(2,1)S(1)} %get-tuple-element.14), kind=kLoop, calls=%fused_computation.4 | loop fusion | flops 31457280 | bytes 41943040 | tf_op jit(solution)/shard_map/stack | solution.py:97
  184.3 8.0 %all-to-all-start = ((bf16[4,5,1,512,1024]{4,3,1,2,0:T(8,128)(2,1)}), bf16[4,5,1,512,1024]{4,3,1,2,0:T(8,128)(2,1)}, u32[]{:S(2)}, u32[]{:S(2)}) async-start(bf16[4,5,1,512,1024]{4,3,1,2,0:T(8,128)(2,1)} %pad_maximum_fusion), calls=%async_computation | async-start | bytes 41943040 | tf_op jit(solution)/shard_map/all_to_all | solution.py:97
  193.1 1.1 slice_multiply_fusion.6
  194.8 446.1 %all-to-all-done = bf16[4,5,1,512,1024]{4,3,1,2,0:T(8,128)(2,1)} async-done(((bf16[4,5,1,512,1024]{4,3,1,2,0:T(8,128)(2,1)}), bf16[4,5,1,512,1024]{4,3,1,2,0:T(8,128)(2,1)}, u32[]{:S(2)}, u32[]{:S(2)}) %all-to-all-start) | async-done | bytes 20971552 | tf_op jit(solution)/shard_map/all_to_all | solution.py:97
  640.9 16.0 %fusion = f32[5,512,1024]{2,1,0:T(8,128)} fusion(bf16[4,5,1,512,1024]{4,3,1,2,0:T(8,128)(2,1)} %all-to-all-done), kind=kLoop, calls=%fused_computation.2 | loop fusion | flops 18350080 | bytes 31457280 | tf_op jit(solution)/shard_map/reduce_sum | solution.py:101
  657.0 7.0 fusion.28
  664.7 23.2 %fusion.1 = f32[5,4,512,1024]{3,2,0,1:T(8,128)} fusion(bf16[4,5,1,512,1024]{4,3,1,2,0:T(8,128)(2,1)} %all-to-all-done, f32[5,512,1024]{2,1,0:T(8,128)S(1)} %copy-done), kind=kLoop, calls=%fused_computation.3 | loop fusion | flops 20971520 | bytes 73400320 | tf_op jit(solution)/shard_map/sub | solution.py:102
  688.0 19.9 %fusion.46 = (f32[512,1024]{1,0:T(8,128)S(1)}, f32[4,512,1024]{2,1,0:T(8,128)}) fusion(f32[4,1024]{1,0:T(4,128)S(1)} %bitcast.81, f32[4,512]{1,0:T(4,128)S(1)} %fusion.35, f32[5,4,512,1024]{3,2,0,1:T(8,128)} %fusion.1), kind=kLoop, calls=%fused_computation.92 | loop fusion | flops 20447232 | bytes 52453376 | tf_op jit(solution)/shard_map/reduce_sum | solution.py:117
  708.1 5.1 multiply_reduce_fusion
  713.7 2.8 sqrt.22
  716.5 3.0 div.75
  719.5 2.6 rsqrt_multiply_fusion
  (46 shorter events, 5.9 us)
Async XLA Ops:
  7.2 118.2 %all-gather.8.cloned.1.call-start = ((), (), s32[]{:S(2)}) async-start(), calls=%async_computation.2 | async-start | bytes 3145728 | tf_op jit(solution)/shard_map/all_gather | solution.py:72
  7.9 117.5 %all-gather.6.cloned.1.call-start = ((), (), s32[]{:S(2)}) async-start(), calls=%async_computation.1 | async-start | bytes 5242880 | tf_op jit(solution)/shard_map/all_gather | solution.py:78
  125.4 10.9 %copy-start.1 = (f32[1024]{0:T(1024)S(1)}, f32[1024]{0:T(1024)}, u32[]{:S(2)}) copy-start(f32[1024]{0:T(1024)} %param.2) | copy-start | bytes 12292
  125.4 10.9 %copy-start.2 = (bf16[1024,2048]{1,0:T(8,128)(2,1)S(1)}, bf16[1024,2048]{1,0:T(8,128)(2,1)}, u32[]{:S(2)}) copy-start(bf16[1024,2048]{1,0:T(8,128)(2,1)} %all-gather.6.cloned.1.call-done) | copy-start | bytes 12582916
  125.4 10.9 %copy-start.3 = (bf16[1024,1024]{1,0:T(8,128)(2,1)S(1)}, bf16[1024,1024]{1,0:T(8,128)(2,1)}, u32[]{:S(2)}) copy-start(bf16[1024,1024]{1,0:T(8,128)(2,1)} %all-gather.8.cloned.1.call-done) | copy-start | bytes 6291460
  184.3 456.7 %all-to-all-start = ((bf16[4,5,1,512,1024]{4,3,1,2,0:T(8,128)(2,1)}), bf16[4,5,1,512,1024]{4,3,1,2,0:T(8,128)(2,1)}, u32[]{:S(2)}, u32[]{:S(2)}) async-start(bf16[4,5,1,512,1024]{4,3,1,2,0:T(8,128)(2,1)} %pad_maximum_fusion), calls=%async_computation | async-start | bytes 41943040 | tf_op jit(solution)/shard_map/all_to_all | solution.py:97
  657.0 7.8 %copy-start = (f32[5,512,1024]{2,1,0:T(8,128)S(1)}, f32[5,512,1024]{2,1,0:T(8,128)}, u32[]{:S(2)}) copy-start(f32[5,512,1024]{2,1,0:T(8,128)} %fusion) | copy-start | bytes 31457284
Sparse Core Ops, SparseCore 0:
  9.5 13.2 all-gather.7
  24.7 54.8 all-gather.5
